TPU v7x, 32 devices: a whole 2x2x4 slice. The times are simulated.
32 devices in a mesh: arc: 2 (over y), trow: 4 (over z), tcol: 4 (over x, core).
Axes of the slice: x: 2, y: 2, z: 4, core: 2. Of those that a mesh axis runs over, the one named last changes fastest.
Arguments:
- design: bfloat16 [1280, 8192], P('arc', 'tcol'), may hold values from -0.25 to 0.25
- local_design: bfloat16 [1280, 128], P('arc'), may hold values from -0.3125 to 0.3125
- lengths: int32 [4], P('arc'), may hold values from 1 to 320, 960 in all
- regularizer: float32 [8192], P(('arc', 'trow')), may hold values from 0.2 to 2
Outputs:
- normal: float32 [8192, 8192], P(('arc', 'trow'), 'tcol')
- panel_factor: float32 [2, 8192, 512], P(None, 'tcol')
Inputs may be any that keep to these rules, and one draw needn't show every extreme that they name: `lengths`: each arc has at least one live row; some arc is full.
All inputs are finite; a program needn't handle non-finite values. No bound on the sum of `lengths` on one device may be relied on, other than what follows from the above.
Results may differ from a plain program's by a relative error of at most 0.003.
Values may be sent and summed in bfloat16 or wider, within the bound.
No kernel may reach another device: no remote copies, remote signals or barrier semaphores. Data moves between devices by JAX's collectives and lax.ppermute only.
A program may use at most 128 MiB of HBM per device.

v0:
```python
import jax
import jax.numpy as jnp
from jax import lax
from jax.sharding import PartitionSpec as P

PANEL = 512
PANELS = 2
ridge = 0.1


def broadcast(block, axis, holder):
    block = jnp.where(lax.axis_index(axis) == holder, block, jnp.zeros_like(block))
    return lax.psum(block, axis)


def project_arcs(design, local_design, lengths):
    arc_count = lengths.shape[0]
    row_count = design.shape[0]
    capacity = row_count // arc_count
    arc_blocks = design.reshape(arc_count, capacity, design.shape[1])
    local_half = local_design.reshape(arc_count, capacity, local_design.shape[1])
    live_rows = jnp.arange(capacity, dtype=jnp.int32)[None, :] < lengths[:, None]
    arc_blocks = jnp.where(live_rows[:, :, None], arc_blocks, jnp.zeros((), design.dtype))
    local_half = jnp.where(live_rows[:, :, None], local_half, jnp.zeros((), local_design.dtype))
    local_normal = jnp.einsum(
        "acl,acm->alm", local_half, local_half, preferred_element_type=jnp.float32
    )
    local_normal = local_normal + ridge * jnp.eye(local_half.shape[2], dtype=jnp.float32)[None]
    local_factor = jnp.linalg.cholesky(local_normal)
    local_cols = local_half.astype(jnp.float32)
    basis_rows = lax.linalg.triangular_solve(
        local_factor, jnp.transpose(local_cols, (0, 2, 1)), left_side=True, lower=True
    )
    basis_rows = basis_rows.astype(jnp.bfloat16)
    loadings = jnp.einsum(
        "alc,acw->alw", basis_rows, arc_blocks, preferred_element_type=jnp.float32
    ).astype(jnp.bfloat16)
    cleaned = arc_blocks.astype(jnp.float32) - jnp.einsum(
        "alc,alw->acw", basis_rows, loadings, preferred_element_type=jnp.float32
    )
    return cleaned.astype(jnp.bfloat16).reshape(row_count, design.shape[1])


def contract_rows(left_rows, right_rows):
    return lax.dot_general(
        left_rows, right_rows, (((0,), (0,)), ((), ())), preferred_element_type=jnp.float32
    )


def per_device(design, local_design, lengths, regularizer):
    row_count, col_width = design.shape
    tile_rows = regularizer.shape[0]
    arc_total = lax.axis_size("arc")
    trow_total = lax.axis_size("trow")
    trow_index = lax.axis_index("trow")
    row_start = (lax.axis_index("arc") * trow_total + trow_index) * tile_rows
    col_start = lax.axis_index("tcol") * col_width
    projected = project_arcs(design, local_design, lengths)
    gathered = lax.all_gather(projected, "tcol", axis=1, tiled=True)
    regrouped = gathered.reshape(row_count, arc_total, trow_total, tile_rows)
    selected = lax.dynamic_slice_in_dim(regrouped, trow_index, 1, 2).reshape(
        row_count, arc_total * tile_rows
    )
    received = lax.all_to_all(selected, "arc", split_axis=1, concat_axis=0, tiled=True)
    normal_block = contract_rows(received, lax.all_gather(projected, "arc", axis=0, tiled=True))
    rows_global = row_start + jnp.arange(tile_rows, dtype=jnp.int32)
    cols_global = col_start + jnp.arange(col_width, dtype=jnp.int32)
    on_diagonal = rows_global[:, None] == cols_global[None, :]
    normal_block = normal_block + jnp.where(
        on_diagonal, regularizer[:, None], jnp.zeros((), jnp.float32)
    )
    panel_factors = []
    for panel_index in range(PANELS):
        lead_col = panel_index * PANEL
        padded_rows = jnp.pad(normal_block, ((PANEL, PANEL), (0, 0)))
        slice_start = jnp.clip(lead_col - row_start + PANEL, 0, tile_rows + PANEL)
        slice_rows = lax.dynamic_slice_in_dim(padded_rows, slice_start, PANEL, 0)
        panel_global = lead_col + jnp.arange(PANEL, dtype=jnp.int32)
        in_tile = (panel_global >= row_start) & (panel_global < row_start + tile_rows)
        own_share = jnp.where(in_tile[:, None], slice_rows, jnp.zeros((), jnp.float32))
        panel_strip = lax.psum(own_share, ("arc", "trow"))
        pivot_block, row_strip = (
            broadcast(panel_strip[:, lead_col : lead_col + PANEL], "tcol", 0),
            broadcast(normal_block[:, lead_col : lead_col + PANEL], "tcol", 0),
        )
        lower_factor = jnp.linalg.cholesky(pivot_block)
        col_factor = lax.linalg.triangular_solve(
            lower_factor, panel_strip, left_side=True, lower=True
        ).T
        row_factor = lax.linalg.triangular_solve(
            lower_factor, row_strip.T, left_side=True, lower=True
        ).T
        col_factor = jnp.where(
            cols_global[:, None] >= lead_col, col_factor, jnp.zeros((), jnp.float32)
        )
        row_factor = jnp.where(
            rows_global[:, None] >= lead_col, row_factor, jnp.zeros((), jnp.float32)
        )
        normal_block = normal_block - jnp.dot(
            row_factor, col_factor.T, precision=lax.Precision.HIGHEST
        )
        panel_factors.append(col_factor)
    return (normal_block, jnp.stack(panel_factors))


def solution(mesh):
    return jax.shard_map(
        per_device,
        mesh=mesh,
        in_specs=(P("arc", "tcol"), P("arc", None), P("arc"), P(("arc", "trow"))),
        out_specs=(P(("arc", "trow"), "tcol"), P(None, "tcol", None)),
        check_vma=False,
    )
```

profile of v0, /device:TPU:0, one launch (start us, length us, event | category | flops | bytes accessed | tf_op | source)
XLA Modules:
  0.0 1101.1 jit_solution(17169129062626182126)
XLA Ops:
  9.6 23.5 %custom-call.33 = f32[2,128,128]{2,1,0:T(8,128)S(1)} custom-call(f32[2,128,128]{2,1,0:T(8,128)S(1)} %fusion.105), custom_call_target="Cholesky" | custom-call | tf_op jit(solution)/shard_map/jit(cholesky)/cholesky | solution.py:29
  33.4 19.7 %custom-call.34 = f32[2,1,128,128]{2,3,1,0:T(8,128)S(1)} custom-call(f32[2,1,128,128]{3,2,1,0:T(8,128)S(1)} %select_bitcast_fusion), custom_call_target="InvertDiagBlocksLowerTriangular" | custom-call | tf_op jit(solution)/shard_map/triangular_solve | solution.py:31
  54.3 4.0 subtract_convert_fusion
  58.4 3.0 copy.64
  62.1 72.3 %all-gather.3.cloned.1.call-done = bf16[640,8192]{0,1:T(8,128)(2,1)} async-done(((bf16[640,2048]{0,1:T(8,128)(2,1)}), bf16[640,8192]{0,1:T(8,128)(2,1)}) %all-gather.3.cloned.1.call-update) | async-done | bytes 10485776 | tf_op jit(solution)/shard_map/all_gather | solution.py:59
  136.4 2.6 copy.65
  139.0 3.9 all-to-all-start
  143.5 87.0 %all-gather.5.cloned.1.call-done = bf16[1280,2048]{1,0:T(8,128)(2,1)} async-done(((bf16[640,2048]{1,0:T(8,128)(2,1)}), bf16[1280,2048]{1,0:T(8,128)(2,1)}) %all-gather.5.cloned.1.call-update) | async-done | bytes 5242896 | tf_op jit(solution)/shard_map/all_gather | solution.py:65
  230.4 8.0 select_add_fusion
  238.5 3.4 copy-done.1
  241.9 3.2 fusion
  245.1 3.2 fusion.23
  248.4 152.4 %all-reduce.10.cloned.1.call-done = f32[512,2048]{0,1:T(8,128)} async-done(((f32[512,2048]{0,1:T(8,128)}), f32[512,2048]{0,1:T(8,128)}) %all-reduce.10.cloned.1.call-update) | async-done | bytes 4194320 | tf_op jit(solution)/shard_map/psum | solution.py:81
  403.2 67.9 %all-reduce.16.cloned.1.call-done = (f32[512,512]{0,1:T(8,128)}, f32[512,1024]{1,0:T(8,128)}) async-done(((f32[512,512]{0,1:T(8,128)}, f32[512,1024]{1,0:T(8,128)}), (f32[512,512]{0,1:T(8,128)}, f32[512,1024]{1,0:T(8,128)})) %all-reduce.16.cloned.1.call-update) | async-done | bytes 3145744 | tf_op jit(solution)/shard_map/psum | solution.py:13
  474.1 11.7 %cholesky.327 = f32[128,128]{1,0:T(8,128)S(1)} custom-call(f32[128,128]{1,0:T(8,128)S(1)} %cholesky.467), custom_call_target="Cholesky" | custom-call | tf_op jit(solution)/shard_map/jit(cholesky)/cholesky | solution.py:86
  486.0 9.8 custom-call.40
  496.5 11.7 %cholesky.346 = f32[128,128]{1,0:T(8,128)S(1)} custom-call(f32[128,128]{1,0:T(8,128)S(1)} %cholesky.471), custom_call_target="Cholesky" | custom-call | tf_op jit(solution)/shard_map/jit(cholesky)/cholesky | solution.py:86
  508.2 10.0 custom-call.41
  518.8 11.7 %cholesky.367 = f32[128,128]{1,0:T(8,128)S(1)} custom-call(f32[128,128]{1,0:T(8,128)S(1)} %cholesky.476), custom_call_target="Cholesky" | custom-call | tf_op jit(solution)/shard_map/jit(cholesky)/cholesky | solution.py:86
  530.6 9.8 custom-call.42
  541.0 11.7 %cholesky.384 = f32[128,128]{1,0:T(8,128)S(1)} custom-call(f32[128,128]{1,0:T(8,128)S(1)} %convolution_subtract_fusion.15), custom_call_target="Cholesky" | custom-call | tf_op jit(solution)/shard_map/jit(cholesky)/cholesky | solution.py:86
  558.4 7.7 while.8
  566.2 39.3 %custom-call.43 = f32[4,128,128]{1,2,0:T(8,128)S(1)} custom-call(f32[4,128,128]{2,1,0:T(8,128)S(1)} %get-tuple-element.33), custom_call_target="InvertDiagBlocksLowerTriangular" | custom-call | tf_op jit(solution)/shard_map/triangular_solve/custom-call.9 | solution.py:90
  608.1 3.0 convolution_subtract_fusion.5
  613.6 4.8 convolution_subtract_fusion.3
  623.1 7.3 fusion.17
  639.3 15.1 %convolution_subtract_fusion.1 = f32[1024,2048]{0,1:T(8,128)S(1)} fusion(f32[1024,2048]{0,1:T(8,128)S(1)} %bitcast.164, f32[128,2048]{0,1:T(8,128)S(1)} %fusion.128, f32[128,2048]{0,1:T(8,128)S(1)} %copy-done.4, f32[128,2048]{0,1:T(8,128)S(1)} %copy-done.3, f32[128,2048]{0,1:T(8,128)S(1)} %copy.71, f32[128,1024]{1,0:T(8,128)S(1)} %fusion.129, ...), kind=kOutput, calls=%fused_computation.14 | convolution fusion | flops 12893290496 | bytes 23071744 | tf_op jit(solution)/shard_map/dot_general | solution.py:99
  654.4 3.4 copy-done
  657.8 3.2 fusion.1
  661.1 3.2 fusion.22
  664.2 153.4 %all-reduce.12.cloned.1.call-done = f32[512,2048]{0,1:T(8,128)} async-done(((f32[512,2048]{0,1:T(8,128)}), f32[512,2048]{0,1:T(8,128)}) %all-reduce.12.cloned.1.call-update) | async-done | bytes 4194320 | tf_op jit(solution)/shard_map/psum | solution.py:81
  820.0 3.6 fusion.21
  823.6 64.4 %all-reduce.14.cloned.1.call-done = (f32[512,512]{0,1:T(8,128)}, f32[512,1024]{1,0:T(8,128)}) async-done(((f32[512,512]{0,1:T(8,128)}, f32[512,1024]{1,0:T(8,128)}), (f32[512,512]{0,1:T(8,128)}, f32[512,1024]{1,0:T(8,128)})) %all-reduce.14.cloned.1.call-update) | async-done | bytes 3145744 | tf_op jit(solution)/shard_map/psum | solution.py:13
  891.0 11.7 %cholesky.399 = f32[128,128]{1,0:T(8,128)S(1)} custom-call(f32[128,128]{1,0:T(8,128)S(1)} %cholesky.480), custom_call_target="Cholesky" | custom-call | tf_op jit(solution)/shard_map/jit(cholesky)/cholesky | solution.py:86
  902.9 9.8 custom-call.45
  913.4 11.7 %cholesky.418 = f32[128,128]{1,0:T(8,128)S(1)} custom-call(f32[128,128]{1,0:T(8,128)S(1)} %cholesky.484), custom_call_target="Cholesky" | custom-call | tf_op jit(solution)/shard_map/jit(cholesky)/cholesky | solution.py:86
  925.1 10.0 custom-call.46
  935.8 11.7 %cholesky.439 = f32[128,128]{1,0:T(8,128)S(1)} custom-call(f32[128,128]{1,0:T(8,128)S(1)} %cholesky.489), custom_call_target="Cholesky" | custom-call | tf_op jit(solution)/shard_map/jit(cholesky)/cholesky | solution.py:86
  947.5 9.8 custom-call.47
  957.9 11.7 %cholesky.456 = f32[128,128]{1,0:T(8,128)S(1)} custom-call(f32[128,128]{1,0:T(8,128)S(1)} %convolution_subtract_fusion.14), custom_call_target="Cholesky" | custom-call | tf_op jit(solution)/shard_map/jit(cholesky)/cholesky | solution.py:86
  975.2 8.3 while.9
  983.6 39.3 %custom-call.48 = f32[4,128,128]{1,2,0:T(8,128)S(1)} custom-call(f32[4,128,128]{2,1,0:T(8,128)S(1)} %get-tuple-element.35), custom_call_target="InvertDiagBlocksLowerTriangular" | custom-call | tf_op jit(solution)/shard_map/triangular_solve/custom-call.9 | solution.py:90
  1025.5 3.0 convolution_subtract_fusion.4
  1031.0 4.8 convolution_subtract_fusion.2
  1040.5 7.5 fusion.14
  1060.6 16.5 %convolution_subtract_fusion = f32[1024,2048]{0,1:T(8,128)} fusion(f32[1024,2048]{0,1:T(8,128)S(1)} %bitcast.162, f32[128,2048]{0,1:T(8,128)S(1)} %fusion.134, f32[128,2048]{0,1:T(8,128)S(1)} %copy-done.7, f32[128,2048]{0,1:T(8,128)S(1)} %copy-done.6, f32[128,2048]{0,1:T(8,128)S(1)} %copy.80, f32[128,1024]{1,0:T(8,128)S(1)} %fusion.135, ...), kind=kOutput, calls=%fused_computation.13 | convolution fusion | flops 12893290496 | bytes 23071744 | tf_op jit(solution)/shard_map/dot_general | solution.py:99
  1077.1 9.1 copy.85
  1086.2 7.8 pad_maximum_fusion
  (168 shorter events, 85.0 us)
Async XLA Ops:
  7.2 127.3 %all-gather.3.cloned.1.call-start = ((), (), s32[]{:S(2)}) async-start(), calls=%async_computation.1 | async-start | bytes 13107200 | tf_op jit(solution)/shard_map/all_gather | solution.py:59
  58.4 3.1 copy-start.2
  61.4 169.1 %all-gather.5.cloned.1.call-start = ((), (), s32[]{:S(2)}) async-start(), calls=%async_computation.2 | async-start | bytes 7864320 | tf_op jit(solution)/shard_map/all_gather | solution.py:65
  136.4 94.1 %copy-start.12 = (f32[1024]{0:T(1024)S(1)}, f32[1024]{0:T(1024)}, u32[]{:S(2)}) copy-start(f32[1024]{0:T(1024)} %param.12) | copy-start | bytes 12292
  139.0 91.4 %all-to-all-start = ((bf16[640,2,1024]{2,0,1:T(8,128)(2,1)}), bf16[640,2,1024]{2,0,1:T(8,128)(2,1)S(1)}, u32[]{:S(2)}, u32[]{:S(2)}) async-start(bf16[640,2,1024]{2,0,1:T(8,128)(2,1)} %bitcast.7), calls=%async_computation | async-start | bytes 5242880 | tf_op jit(solution)/shard_map/all_to_all | solution.py:64
  142.9 257.8 %all-reduce.10.cloned.1.call-start = ((), (), s32[]{:S(2)}) async-start(), calls=%async_computation.3 | async-start | bytes 8388608 | tf_op jit(solution)/shard_map/psum | solution.py:81
  238.5 3.4 copy-start.1
  245.1 226.0 %all-reduce.16.cloned.1.call-start = ((), (), s32[]{:S(2)}) async-start(), calls=%async_computation.6 | async-start | bytes 6291456 | tf_op jit(solution)/shard_map/psum | solution.py:13
  403.0 414.6 %all-reduce.12.cloned.1.call-start = ((), (), s32[]{:S(2)}) async-start(), calls=%async_computation.4 | async-start | bytes 8388608 | tf_op jit(solution)/shard_map/psum | solution.py:81
  566.2 42.0 %copy-start.9 = (f32[512,512]{1,0:T(8,128)}, f32[512,512]{1,0:T(8,128)S(1)}, u32[]{:S(2)}) copy-start(f32[512,512]{1,0:T(8,128)S(1)} %get-tuple-element.210) | copy-start | bytes 3145732
  623.1 8.3 copy-start.10
  623.1 16.2 %slice-start.2 = ((s8[8388608]{0:T(1024)(128)(4,1)}), s8[4194304]{0:T(1024)(128)(4,1)S(1)}, s32[]{:S(2)}) async-start(s8[8388608]{0:T(1024)(128)(4,1)} %bitcast.163), calls=%async_computation.9 | async-start | bytes 8388608
  631.4 7.9 copy-start.5
  632.1 7.2 slice-start.3
  633.7 5.7 copy-start.3
  633.7 5.7 copy-start.4
  654.4 3.4 copy-start
  661.0 227.0 %all-reduce.14.cloned.1.call-start = ((), (), s32[]{:S(2)}) async-start(), calls=%async_computation.5 | async-start | bytes 6291456 | tf_op jit(solution)/shard_map/psum | solution.py:13
  983.6 42.0 %copy-start.8 = (f32[512,512]{1,0:T(8,128)}, f32[512,512]{1,0:T(8,128)S(1)}, u32[]{:S(2)}) copy-start(f32[512,512]{1,0:T(8,128)S(1)} %get-tuple-element.209) | copy-start | bytes 3145732
  1040.5 8.6 copy-start.11
  1051.1 5.8 copy-start.6
  1051.1 5.8 copy-start.7
  1051.7 7.5 slice-start
  1056.9 3.7 slice-start.1
Sparse Core Ops, SparseCore 0:
  61.5 72.8 all-gather.2
  136.5 93.8 all-gather.4
  245.2 155.4 all-reduce.9
  403.6 67.4 all-reduce.15
  661.1 156.4 all-reduce.11
  820.5 67.4 all-reduce.13
where the time goes:
time: 1110 us; the launch traced here: 1100 us
  waiting for transfers between devices  598 us (54%)
  other arithmetic  316 us (28%)
  matrix products  109 us (10%)
  local copies, waits for them, and re-layouts  52.6 us (5%)
  between operations  20.3 us (2%)
    psum x2, waiting for transfers between devices, per_device(): panel_strip = lax.psum(own_share, ('arc', 'trow'))  306 us
    another operation x30, other arithmetic, per_device(): lower_factor = jnp.linalg.cholesky(pivot_block)  158 us
    psum x2, waiting for transfers between devices, broadcast(): return lax.psum(block, axis)  132 us
    all_gather x1, waiting for transfers between devices, per_device(): lax.all_gather(projected, 'arc', axis=0, tiled=True)  87 us
    another operation x5, other arithmetic, per_device(): lax.linalg.triangular_solve(lower_factor, row_strip.T, left_side=True, lo...  79.5 us
    all_gather x1, waiting for transfers between devices, per_device(): gathered = lax.all_gather(projected, 'tcol', axis=1, tiled=True)  72.3 us
    another operation x14, matrix products, per_device(): lax.linalg.triangular_solve(lower_factor, panel_strip, left_side=True, lo...  43.5 us
    dot_general x2, matrix products, per_device(): jnp.dot(row_factor, col_factor.T, precision=lax.Precision.HIGHEST)  31.6 us
  transfers between devices with their start and end apart: 7, of which 6 were waited for; matrix products, arithmetic and copies ran while one was open for 1% of the time, Pallas kernels for 0%

commit v1 on v0

--- a/solution.py
+++ b/solution.py
@@ -78,7 +78,7 @@
         panel_global = lead_col + jnp.arange(PANEL, dtype=jnp.int32)
         in_tile = (panel_global >= row_start) & (panel_global < row_start + tile_rows)
         own_share = jnp.where(in_tile[:, None], slice_rows, jnp.zeros((), jnp.float32))
-        panel_strip = lax.psum(own_share, ("arc", "trow"))
+        panel_strip = lax.psum(lax.psum(own_share, "trow"), "arc")
         pivot_block, row_strip = (
             broadcast(panel_strip[:, lead_col : lead_col + PANEL], "tcol", 0),
             broadcast(normal_block[:, lead_col : lead_col + PANEL], "tcol", 0),

time: 1110 us -> 1330 us (1.20)
  waiting for transfers between devices: 598 us -> 816 us
    psum x2 -> x4, waiting for transfers between devices: 306 us -> 521 us  [per_device(): panel_strip = lax.psum(lax.psum(own_share, 'trow'), 'arc')]
  transfers between devices with their start and end apart: 7 -> 9, of which waited for: 6 -> 8; matrix products, arithmetic and copies ran while one was open for 1% -> 1% of each run, Pallas kernels for 0% -> 0%
where the time goes in v1:
time: 1330 us; the launch traced here: 1320 us
  waiting for transfers between devices  816 us (61%)
  other arithmetic  316 us (24%)
  matrix products  109 us (8%)
  local copies, waits for them, and re-layouts  52.6 us (4%)
  between operations  20.3 us (2%)
    psum x4, waiting for transfers between devices, per_device(): panel_strip = lax.psum(lax.psum(own_share, 'trow'), 'arc')  521 us
    another operation x30, other arithmetic, per_device(): lower_factor = jnp.linalg.cholesky(pivot_block)  158 us
    psum x2, waiting for transfers between devices, broadcast(): return lax.psum(block, axis)  134 us
    all_gather x1, waiting for transfers between devices, per_device(): lax.all_gather(projected, 'arc', axis=0, tiled=True)  87 us
    another operation x5, other arithmetic, per_device(): lax.linalg.triangular_solve(lower_factor, row_strip.T, left_side=True, lo...  79.5 us
    all_gather x1, waiting for transfers between devices, per_device(): gathered = lax.all_gather(projected, 'tcol', axis=1, tiled=True)  72.3 us
    another operation x14, matrix products, per_device(): lax.linalg.triangular_solve(lower_factor, panel_strip, left_side=True, lo...  43.5 us
    dot_general x2, matrix products, per_device(): jnp.dot(row_factor, col_factor.T, precision=lax.Precision.HIGHEST)  31.6 us
  transfers between devices with their start and end apart: 9, of which 8 were waited for; matrix products, arithmetic and copies ran while one was open for 1% of the time, Pallas kernels for 0%

profile of v1, /device:TPU:0, one launch (start us, length us, event | category | flops | bytes accessed | tf_op | source)
XLA Modules:
  0.0 1319.0 jit_solution(3691318049182748165)
XLA Ops:
  9.6 23.5 %custom-call.33 = f32[2,128,128]{2,1,0:T(8,128)S(1)} custom-call(f32[2,128,128]{2,1,0:T(8,128)S(1)} %fusion.105), custom_call_target="Cholesky" | custom-call | tf_op jit(solution)/shard_map/jit(cholesky)/cholesky | solution.py:29
  33.4 19.7 %custom-call.34 = f32[2,1,128,128]{2,3,1,0:T(8,128)S(1)} custom-call(f32[2,1,128,128]{3,2,1,0:T(8,128)S(1)} %select_bitcast_fusion), custom_call_target="InvertDiagBlocksLowerTriangular" | custom-call | tf_op jit(solution)/shard_map/triangular_solve | solution.py:31
  54.3 4.0 subtract_convert_fusion
  62.1 72.3 %all-gather.3.cloned.1.call-done = bf16[640,8192]{0,1:T(8,128)(2,1)} async-done(((bf16[640,2048]{0,1:T(8,128)(2,1)}), bf16[640,8192]{0,1:T(8,128)(2,1)}) %all-gather.3.cloned.1.call-update) | async-done | bytes 10485776 | tf_op jit(solution)/shard_map/all_gather | solution.py:59
  139.0 3.9 all-to-all-start
  143.5 87.0 %all-gather.5.cloned.1.call-done = bf16[1280,2048]{1,0:T(8,128)(2,1)} async-done(((bf16[640,2048]{1,0:T(8,128)(2,1)}), bf16[1280,2048]{1,0:T(8,128)(2,1)}) %all-gather.5.cloned.1.call-update) | async-done | bytes 5242896 | tf_op jit(solution)/shard_map/all_gather | solution.py:65
  230.4 8.0 select_add_fusion
  238.5 3.4 copy-done.1
  241.9 3.2 fusion
  245.1 154.2 %all-reduce.12.cloned.1.call-done = f32[512,2048]{0,1:T(8,128)} async-done(((f32[512,2048]{0,1:T(8,128)}), f32[512,2048]{0,1:T(8,128)}) %all-reduce.12.cloned.1.call-update) | async-done | bytes 4194320 | tf_op jit(solution)/shard_map/psum | solution.py:81
  399.4 3.2 fusion.23
  402.6 105.9 %all-reduce.14.cloned.1.call-done = f32[512,2048]{0,1:T(8,128)} async-done(((f32[512,2048]{0,1:T(8,128)}), f32[512,2048]{0,1:T(8,128)}) %all-reduce.14.cloned.1.call-update) | async-done | bytes 4194320 | tf_op jit(solution)/shard_map/psum | solution.py:81
  511.0 68.9 %all-reduce.22.cloned.1.call-done = (f32[512,512]{0,1:T(8,128)}, f32[512,1024]{1,0:T(8,128)}) async-done(((f32[512,512]{0,1:T(8,128)}, f32[512,1024]{1,0:T(8,128)}), (f32[512,512]{0,1:T(8,128)}, f32[512,1024]{1,0:T(8,128)})) %all-reduce.22.cloned.1.call-update) | async-done | bytes 3145744 | tf_op jit(solution)/shard_map/psum | solution.py:13
  582.9 11.7 cholesky.327
  594.8 9.8 custom-call.40
  605.3 11.7 cholesky.346
  617.0 10.0 custom-call.41
  627.6 11.7 cholesky.367
  639.4 9.8 custom-call.42
  649.8 11.7 cholesky.384
  667.2 7.7 while.8
  675.0 39.3 %custom-call.43 = f32[4,128,128]{1,2,0:T(8,128)S(1)} custom-call(f32[4,128,128]{2,1,0:T(8,128)S(1)} %get-tuple-element.33), custom_call_target="InvertDiagBlocksLowerTriangular" | custom-call | tf_op jit(solution)/shard_map/triangular_solve/custom-call.9 | solution.py:90
  716.9 3.0 convolution_subtract_fusion.5
  722.4 4.8 convolution_subtract_fusion.3
  731.9 7.3 fusion.17
  748.1 15.1 %convolution_subtract_fusion.1 = f32[1024,2048]{0,1:T(8,128)S(1)} fusion(f32[1024,2048]{0,1:T(8,128)S(1)} %bitcast.164, f32[128,2048]{0,1:T(8,128)S(1)} %fusion.128, f32[128,2048]{0,1:T(8,128)S(1)} %copy-done.4, f32[128,2048]{0,1:T(8,128)S(1)} %copy-done.3, f32[128,2048]{0,1:T(8,128)S(1)} %copy.71, f32[128,1024]{1,0:T(8,128)S(1)} %fusion.129, ...), kind=kOutput, calls=%fused_computation.14 | convolution fusion | flops 12893290496 | bytes 23071744 | tf_op jit(solution)/shard_map/dot_general | solution.py:99
  763.2 3.4 copy-done
  766.6 3.2 fusion.1
  769.9 155.2 %all-reduce.16.cloned.1.call-done = f32[512,2048]{0,1:T(8,128)} async-done(((f32[512,2048]{0,1:T(8,128)}), f32[512,2048]{0,1:T(8,128)}) %all-reduce.16.cloned.1.call-update) | async-done | bytes 4194320 | tf_op jit(solution)/shard_map/psum | solution.py:81
  925.1 3.2 fusion.22
  928.3 106.1 %all-reduce.18.cloned.1.call-done = f32[512,2048]{0,1:T(8,128)} async-done(((f32[512,2048]{0,1:T(8,128)}), f32[512,2048]{0,1:T(8,128)}) %all-reduce.18.cloned.1.call-update) | async-done | bytes 4194320 | tf_op jit(solution)/shard_map/psum | solution.py:81
  1036.9 3.6 fusion.21
  1040.4 65.5 %all-reduce.20.cloned.1.call-done = (f32[512,512]{0,1:T(8,128)}, f32[512,1024]{1,0:T(8,128)}) async-done(((f32[512,512]{0,1:T(8,128)}, f32[512,1024]{1,0:T(8,128)}), (f32[512,512]{0,1:T(8,128)}, f32[512,1024]{1,0:T(8,128)})) %all-reduce.20.cloned.1.call-update) | async-done | bytes 3145744 | tf_op jit(solution)/shard_map/psum | solution.py:13
  1108.9 11.7 cholesky.399
  1120.8 9.8 custom-call.45
  1131.3 11.7 cholesky.418
  1143.1 10.0 custom-call.46
  1153.7 11.7 cholesky.439
  1165.4 9.8 custom-call.47
  1175.9 11.7 cholesky.456
  1193.1 8.3 while.9
  1201.5 39.3 %custom-call.48 = f32[4,128,128]{1,2,0:T(8,128)S(1)} custom-call(f32[4,128,128]{2,1,0:T(8,128)S(1)} %get-tuple-element.35), custom_call_target="InvertDiagBlocksLowerTriangular" | custom-call | tf_op jit(solution)/shard_map/triangular_solve/custom-call.9 | solution.py:90
  1243.5 3.0 convolution_subtract_fusion.4
  1248.9 4.8 convolution_subtract_fusion.2
  1258.4 7.5 fusion.14
  1278.5 16.5 %convolution_subtract_fusion = f32[1024,2048]{0,1:T(8,128)} fusion(f32[1024,2048]{0,1:T(8,128)S(1)} %bitcast.162, f32[128,2048]{0,1:T(8,128)S(1)} %fusion.134, f32[128,2048]{0,1:T(8,128)S(1)} %copy-done.7, f32[128,2048]{0,1:T(8,128)S(1)} %copy-done.6, f32[128,2048]{0,1:T(8,128)S(1)} %copy.80, f32[128,1024]{1,0:T(8,128)S(1)} %fusion.135, ...), kind=kOutput, calls=%fused_computation.13 | convolution fusion | flops 12893290496 | bytes 23071744 | tf_op jit(solution)/shard_map/dot_general | solution.py:99
  1295.0 9.1 copy.85
  1304.1 7.8 pad_maximum_fusion
  (174 shorter events, 90.8 us)
Async XLA Ops:
  7.2 127.3 %all-gather.3.cloned.1.call-start = ((), (), s32[]{:S(2)}) async-start(), calls=%async_computation.1 | async-start | bytes 13107200 | tf_op jit(solution)/shard_map/all_gather | solution.py:59
  58.4 3.1 copy-start.2
  61.4 169.1 %all-gather.5.cloned.1.call-start = ((), (), s32[]{:S(2)}) async-start(), calls=%async_computation.2 | async-start | bytes 7864320 | tf_op jit(solution)/shard_map/all_gather | solution.py:65
  136.4 94.1 %copy-start.12 = (f32[1024]{0:T(1024)S(1)}, f32[1024]{0:T(1024)}, u32[]{:S(2)}) copy-start(f32[1024]{0:T(1024)} %param.12) | copy-start | bytes 12292
  139.0 91.4 %all-to-all-start = ((bf16[640,2,1024]{2,0,1:T(8,128)(2,1)}), bf16[640,2,1024]{2,0,1:T(8,128)(2,1)S(1)}, u32[]{:S(2)}, u32[]{:S(2)}) async-start(bf16[640,2,1024]{2,0,1:T(8,128)(2,1)} %bitcast.7), calls=%async_computation | async-start | bytes 5242880 | tf_op jit(solution)/shard_map/all_to_all | solution.py:64
  142.9 256.4 %all-reduce.12.cloned.1.call-start = ((), (), s32[]{:S(2)}) async-start(), calls=%async_computation.3 | async-start | bytes 8388608 | tf_op jit(solution)/shard_map/psum | solution.py:81
  238.5 3.4 copy-start.1
  245.1 263.4 %all-reduce.14.cloned.1.call-start = ((), (), s32[]{:S(2)}) async-start(), calls=%async_computation.4 | async-start | bytes 8388608 | tf_op jit(solution)/shard_map/psum | solution.py:81
  399.4 180.5 %all-reduce.22.cloned.1.call-start = ((), (), s32[]{:S(2)}) async-start(), calls=%async_computation.8 | async-start | bytes 6291456 | tf_op jit(solution)/shard_map/psum | solution.py:13
  510.9 414.2 %all-reduce.16.cloned.1.call-start = ((), (), s32[]{:S(2)}) async-start(), calls=%async_computation.5 | async-start | bytes 8388608 | tf_op jit(solution)/shard_map/psum | solution.py:81
  675.0 42.0 %copy-start.9 = (f32[512,512]{1,0:T(8,128)}, f32[512,512]{1,0:T(8,128)S(1)}, u32[]{:S(2)}) copy-start(f32[512,512]{1,0:T(8,128)S(1)} %get-tuple-element.212) | copy-start | bytes 3145732
  731.9 8.3 copy-start.10
  731.9 16.2 %slice-start.2 = ((s8[8388608]{0:T(1024)(128)(4,1)}), s8[4194304]{0:T(1024)(128)(4,1)S(1)}, s32[]{:S(2)}) async-start(s8[8388608]{0:T(1024)(128)(4,1)} %bitcast.163), calls=%async_computation.11 | async-start | bytes 8388608
  740.2 7.9 copy-start.5
  740.9 7.2 slice-start.3
  742.5 5.7 copy-start.3
  742.5 5.7 copy-start.4
  763.2 3.4 copy-start
  769.8 264.6 %all-reduce.18.cloned.1.call-start = ((), (), s32[]{:S(2)}) async-start(), calls=%async_computation.6 | async-start | bytes 8388608 | tf_op jit(solution)/shard_map/psum | solution.py:81
  925.1 180.8 %all-reduce.20.cloned.1.call-start = ((), (), s32[]{:S(2)}) async-start(), calls=%async_computation.7 | async-start | bytes 6291456 | tf_op jit(solution)/shard_map/psum | solution.py:13
  1201.5 42.0 %copy-start.8 = (f32[512,512]{1,0:T(8,128)}, f32[512,512]{1,0:T(8,128)S(1)}, u32[]{:S(2)}) copy-start(f32[512,512]{1,0:T(8,128)S(1)} %get-tuple-element.211) | copy-start | bytes 3145732
  1258.4 8.6 copy-start.11
  1269.0 5.8 copy-start.6
  1269.0 5.8 copy-start.7
  1269.7 7.5 slice-start
  1274.8 3.7 slice-start.1
Sparse Core Ops, SparseCore 0:
  61.5 72.8 all-gather.2
  136.5 93.8 all-gather.4
  245.2 154.0 all-reduce.11
  401.6 106.8 all-reduce.13
  511.4 68.4 all-reduce.21
  769.9 155.0 all-reduce.15
  927.5 106.8 all-reduce.17
  1037.4 68.4 all-reduce.19
